TPU v7x, 256 devices: a whole 4x4x8 slice. The times are simulated.
256 devices in a mesh: task: 8 (over x_hi, y), mp: 32 (over x_lo, z, core).
Axes of the slice: x: 4 (x_hi: 2, x_lo: 2; x = x_hi * 2 + x_lo), y: 4, z: 8, core: 2. Of those that a mesh axis runs over, the one named last changes fastest.
Arguments:
- hidden: bfloat16 [8, 2048, 8192], P('task', 'mp'), may hold values from -6 to 6
- gain: float32 [8192], replicated, may hold values from 0.25 to 1.75
- tau: bfloat16 [8, 8192, 1024], P('task', 'mp'), may hold values from -0.0625 to 0.0625
- coeff: float32 [8, 8192, 1024], P('task', 'mp'), may hold values from 0.1 to 1
- counts: int32 [8], P('task'), may hold values from 683 to 2048, as said below
- positions: int32 [8, 2048], P('task', 'mp'), may hold values from 0 to 2047
Outputs:
- grad_coeff: float32 [8, 8192, 1024], P('task', 'mp')
- loss: float32 [], replicated
Inputs may be any that keep to these rules, and one draw needn't show every extreme that they name: `counts`: counts lie between a third of 2048 and 2048; some task has exactly 2048 in every draw. Rows at or past a task's count are not live.
All inputs are finite; a program needn't handle non-finite values.
Results may differ from a plain program's by a relative error of at most 0.0044.
The roundings to bfloat16 on the way count: a program that leaves them out, or rounds other values in their place, can miss the bound.
Values may be sent and summed in bfloat16 or wider, within the bound.
A program may use at most 64 MiB of HBM per device.

v0:
```python
import jax
import jax.numpy as jnp
from jax import lax
from jax.sharding import Mesh
from jax.sharding import PartitionSpec as P

HEAD = 128
MP = ("mp_0", "mp_1", "mp_2")
TASK = ("task_0", "task_1")
TASK_MP = ("task_0", "task_1", "mp_0", "mp_1", "mp_2")


def cut_along(value, dim, length):
    before, after = (value.shape[:dim], value.shape[dim + 1 :])
    return jnp.moveaxis(value.reshape(*before, length, -1, *after), dim, 0)


def scatter_pairs(value, chips, core, dim):
    sizes = (lax.axis_size(chips), lax.axis_size(core))
    tiles = cut_along(value, dim, sizes[0] * sizes[1])
    inside = tiles.shape[1:]
    tiles = tiles.reshape(*sizes, *inside).swapaxes(0, 1).reshape(-1, *inside)
    tiles = lax.psum_scatter(tiles, core, scatter_dimension=0, tiled=True)
    return lax.psum_scatter(tiles, chips, scatter_dimension=0, tiled=True)[0]


def by_axis(value, axes):
    for axis in axes:
        value = lax.psum(value, axis)
    return value


def rotary_tables(positions, head):
    index = jnp.arange(head // 2).astype(jnp.float32)
    freq = jnp.exp(-jnp.log(jnp.float32(1000000.0)) * 2.0 * index / head)
    angle = positions.astype(jnp.float32)[:, None] * freq[None, :]
    return (jnp.cos(angle), jnp.sin(angle))


def rotate(values, cosine, sine, sign, head):
    count = values.shape[0]
    width = values.shape[1]
    shaped = values.reshape(count, width // head, 2, head // 2)
    first = shaped[:, :, 0, :]
    second = shaped[:, :, 1, :]
    cosine = cosine[:, None, :]
    sine = sine[:, None, :] * sign
    out_first = first * cosine - second * sine
    out_second = second * cosine + first * sine
    return jnp.stack([out_first, out_second], axis=2).reshape(count, width)


def local(hidden, gain, tau, coeff, counts, positions):
    rows = hidden[0].astype(jnp.float32)
    width = rows.shape[1]
    keys = tau.shape[2]
    rows_local = rows.shape[0]
    inverse = 1.0 / jnp.sqrt(jnp.mean(rows * rows, axis=1, keepdims=True) + 1e-06)
    normed = (rows * inverse * gain[None, :]).astype(jnp.bfloat16)
    columns = lax.all_to_all(normed, MP, split_axis=1, concat_axis=0, tiled=True)
    tau_local = tau[0].astype(jnp.float32)
    mixed = lax.psum(coeff[0] * tau_local, TASK)
    merged = mixed.astype(jnp.bfloat16)
    teacher = tau[0]
    block = columns
    gap = scatter_pairs(
        jnp.dot(block, merged, preferred_element_type=jnp.float32)
        - jnp.dot(block, teacher, preferred_element_type=jnp.float32),
        ("mp_0", "mp_1"),
        "mp_2",
        0,
    )
    first_row = lax.axis_index(MP) * rows_local
    cosine, sine = rotary_tables(positions[0], HEAD)
    err = rotate(gap, cosine, sine, 1.0, HEAD)
    row_ids = first_row + jnp.arange(rows_local)
    live = (row_ids < counts[0]).astype(jnp.float32)[:, None]
    scale = 1.0 / (counts[0].astype(jnp.float32) * keys)
    partial_loss = jnp.sum(live * err * err) * scale
    back = rotate(2.0 * scale * live * err, cosine, sine, -1.0, HEAD).astype(jnp.bfloat16)
    block = columns
    local_grad = lax.dot_general(
        block,
        lax.all_gather(back, MP, axis=0, tiled=True),
        (((0,), (0,)), ((), ())),
        preferred_element_type=jnp.float32,
    )
    wgrad = lax.psum(local_grad, TASK)
    loss = by_axis(partial_loss, TASK_MP)
    grad_coeff = width * keys * tau_local * wgrad
    return (grad_coeff[None, :, :], loss)


def solution(mesh):
    split = Mesh(mesh.devices.reshape(2, 4, 2, 8, 2), ("task_0", "task_1", "mp_0", "mp_1", "mp_2"))
    placed = (P(TASK, MP, None), P(), P(TASK, MP, None), P(TASK, MP, None), P(TASK), P(TASK, MP))
    return jax.shard_map(
        local, mesh=split, in_specs=placed, out_specs=(P(TASK, MP, None), P()), check_vma=False
    )
```

profile of v0, /device:TPU:32, one launch (start us, length us, event | category | flops | bytes accessed | tf_op | source)
XLA Modules:
  0.0 391.9 jit_solution(13827501548182623606)
XLA Ops:
  7.2 1.5 multiply_reduce_fusion
  8.7 1.5 copy.13
  10.6 1.6 copy.11
  12.1 9.7 %all-to-all-start = ((bf16[64,32,256]{2,0,1:T(8,128)(2,1)}), bf16[64,32,256]{2,0,1:T(8,128)(2,1)S(1)}, u32[]{:S(2)}, u32[]{:S(2)}) async-start(bf16[64,32,256]{2,0,1:T(8,128)(2,1)} %copy.11), calls=%async_computation | async-start | bytes 2097152 | tf_op jit(solution)/shard_map/all_to_all | solution.py:60
  21.8 1.4 convert_multiply_fusion
  23.2 81.8 %all-reduce.4 = bf16[256,1024]{1,0:T(8,128)(2,1)S(1)} all-reduce(f32[256,1024]{1,0:T(8,128)S(1)} %convert_multiply_fusion), channel_id=1, replica_groups=mesh['task_0'=2,'task_1'=4,'mp_0'=2,'mp_1'=8,'mp_2'=2] {'task_0','task_1'}, use_global_device_ids=true, to_apply=%region_1.0 | all-reduce | flops 262144 | bytes 1572864 | tf_op jit(solution)/shard_map/psum | solution.py:62
  105.0 1.3 fusion.9
  106.3 1.3 convolution_subtract_fusion
  107.6 4.1 %copy.12 = f32[16,2,64,1024]{3,2,0,1:T(8,128)} copy(f32[16,2,64,1024]{3,2,1,0:T(8,128)S(1)} %bitcast.36) | data formatting | bytes 16777216 | tf_op jit(solution)/shard_map/reshape;reshape | solution.py:22
  111.7 19.8 %reduce-scatter.3.cloned.1.call-done = f32[16,64,1024]{2,1,0:T(8,128)} async-done(((f32[32,64,1024]{2,1,0:T(8,128)}), f32[16,64,1024]{2,1,0:T(8,128)}) %reduce-scatter.3.cloned.1.call-update) | async-done | bytes 4194320 | tf_op jit(solution)/shard_map/reduce_scatter | solution.py:23
  132.6 81.7 %reduce-scatter.5.cloned.1.call-done = f32[1,64,1024]{2,1,0:T(8,128)} async-done(((f32[16,64,1024]{2,1,0:T(8,128)}), f32[1,64,1024]{2,1,0:T(8,128)}) %reduce-scatter.5.cloned.1.call-update) | async-done | bytes 262160 | tf_op jit(solution)/shard_map/reduce_scatter | solution.py:24
  214.2 1.3 reshape_squeeze.3
  216.2 1.8 fusion.4
  218.6 0.7 pad_maximum_fusion.1
  219.3 0.9 convert_element_type.62
  220.3 64.3 %all-gather.2.cloned.1.call-done = bf16[2048,1024]{1,0:T(8,128)(2,1)} async-done(((bf16[64,1024]{1,0:T(8,128)(2,1)}), bf16[2048,1024]{1,0:T(8,128)(2,1)}) %all-gather.2.cloned.1.call-update) | async-done | bytes 4194320 | tf_op jit(solution)/shard_map/all_gather | solution.py:84
  284.5 4.4 %fusion.8 = f32[256,1024]{1,0:T(8,128)} fusion(bf16[2048,256]{1,0:T(8,128)(2,1)S(1)} %bitcast.40, bf16[2048,1024]{1,0:T(8,128)(2,1)} %all-gather.2.cloned.1.call-done), kind=kOutput, calls=%fused_computation.30 | convolution fusion | flops 1073741824 | bytes 6291456 | tf_op jit(solution)/shard_map/dot_general | solution.py:82
  289.6 6.9 %psum.51 = f32[]{:T(128)} all-reduce(f32[]{:T(128)S(6)} %mul.221), channel_id=1, replica_groups=mesh['task_0'=2,'task_1'=4,'mp_0'=2,'mp_1'=8,'mp_2'=2] {'task_0'}, use_global_device_ids=true, to_apply=%region_6.0 | all-reduce | flops 1 | bytes 8 | tf_op jit(solution)/shard_map/psum | solution.py:29
  296.6 11.5 %psum.52 = f32[]{:T(128)} all-reduce(f32[]{:T(128)} %psum.51), channel_id=1, replica_groups=mesh['task_0'=2,'task_1'=4,'mp_0'=2,'mp_1'=8,'mp_2'=2] {'task_1'}, use_global_device_ids=true, to_apply=%region_7.0 | all-reduce | flops 1 | bytes 8 | tf_op jit(solution)/shard_map/psum | solution.py:29
  308.1 5.5 %psum.53 = f32[]{:T(128)} all-reduce(f32[]{:T(128)} %psum.52), channel_id=1, replica_groups=mesh['task_0'=2,'task_1'=4,'mp_0'=2,'mp_1'=8,'mp_2'=2] {'mp_0'}, use_global_device_ids=true, to_apply=%region_8.0 | all-reduce | flops 1 | bytes 8 | tf_op jit(solution)/shard_map/psum | solution.py:29
  313.6 15.9 %psum.54 = f32[]{:T(128)} all-reduce(f32[]{:T(128)} %psum.53), channel_id=1, replica_groups=mesh['task_0'=2,'task_1'=4,'mp_0'=2,'mp_1'=8,'mp_2'=2] {'mp_1'}, use_global_device_ids=true, to_apply=%region_9.0 | all-reduce | flops 1 | bytes 8 | tf_op jit(solution)/shard_map/psum | solution.py:29
  329.5 3.1 psum.55
  332.5 50.5 %all-reduce.3.cloned.1.call-done = f32[256,1024]{1,0:T(8,128)} async-done(((f32[256,1024]{1,0:T(8,128)}), f32[256,1024]{1,0:T(8,128)}) %all-reduce.3.cloned.1.call-update) | async-done | bytes 1048592 | tf_op jit(solution)/shard_map/psum | solution.py:88
  383.0 2.4 fusion.3
  (25 shorter events, 2.0 us)
Async XLA Ops:
  7.2 3.1 copy-start.1
  10.2 11.6 %copy-start = (bf16[1,256,1024]{2,1,0:T(8,128)(2,1)S(1)}, bf16[1,256,1024]{2,1,0:T(8,128)(2,1)}, u32[]{:S(2)}) copy-start(bf16[1,256,1024]{2,1,0:T(8,128)(2,1)} %param.8) | copy-start | bytes 1572868
  12.1 92.9 %all-to-all-start = ((bf16[64,32,256]{2,0,1:T(8,128)(2,1)}), bf16[64,32,256]{2,0,1:T(8,128)(2,1)S(1)}, u32[]{:S(2)}, u32[]{:S(2)}) async-start(bf16[64,32,256]{2,0,1:T(8,128)(2,1)} %copy.11), calls=%async_computation | async-start | bytes 2097152 | tf_op jit(solution)/shard_map/all_to_all | solution.py:60
  21.8 109.8 %reduce-scatter.3.cloned.1.call-start = ((), (), s32[]{:S(2)}) async-start(), calls=%async_computation.3 | async-start | bytes 12582912 | tf_op jit(solution)/shard_map/reduce_scatter | solution.py:23
  111.7 20.7 %copy-start.2 = (s32[1,64]{1,0:T(1,128)S(1)}, s32[1,64]{1,0:T(1,128)}, u32[]{:S(2)}) copy-start(s32[1,64]{1,0:T(1,128)} %param.11) | copy-start | bytes 772
  111.7 102.6 %reduce-scatter.5.cloned.1.call-start = ((), (), s32[]{:S(2)}) async-start(), calls=%async_computation.4 | async-start | bytes 4456448 | tf_op jit(solution)/shard_map/reduce_scatter | solution.py:24
  131.6 153.0 %all-gather.2.cloned.1.call-start = ((), (), s32[]{:S(2)}) async-start(), calls=%async_computation.5 | async-start | bytes 4325376 | tf_op jit(solution)/shard_map/all_gather | solution.py:84
  220.2 162.8 %all-reduce.3.cloned.1.call-start = ((), (), s32[]{:S(2)}) async-start(), calls=%async_computation.6 | async-start | bytes 2097152 | tf_op jit(solution)/shard_map/psum | solution.py:88
Sparse Core Ops, SparseCore 0:
  111.8 19.7 reduce-scatter.2
  134.1 80.0 reduce-scatter.4
  220.3 64.1 all-gather.1
  289.1 93.8 all-reduce.2
where the time goes:
time: 392 us
  waiting for transfers between devices  216 us (55%)
  blocking collectives  125 us (32%)
  between operations  15.3 us (4%)
  starting transfers between devices  9.82 us (3%)
  other arithmetic  9.5 us (2%)
  local copies, waits for them, and re-layouts  9.36 us (2%)
  matrix products  6.95 us (2%)
    psum x1, blocking collectives, local(): mixed = lax.psum(coeff[0] * tau_local, TASK)  81.8 us
    reduce_scatter x1, waiting for transfers between devices, scatter_pairs(): return lax.psum_scatter(tiles, chips, scatter_dimension=0, tiled=True)[0]  81.7 us
    all_gather x1, waiting for transfers between devices, local(): lax.all_gather(back, MP, axis=0, tiled=True)  64.3 us
    psum x1, waiting for transfers between devices, local(): wgrad = lax.psum(local_grad, TASK)  50.5 us
    psum x5, blocking collectives, by_axis(): value = lax.psum(value, axis)  42.9 us
    reduce_scatter x1, waiting for transfers between devices, scatter_pairs(): tiles = lax.psum_scatter(tiles, core, scatter_dimension=0, tiled=True)  19.8 us
    all_to_all x1, starting transfers between devices, local(): lax.all_to_all(normed, MP, split_axis=1, concat_axis=0, tiled=True)  9.65 us
  transfers between devices with their start and end apart: 5, of which 4 were waited for; matrix products, arithmetic and copies ran while one was open for 0% of the time, Pallas kernels for 0%

commit v1 on v0

--- a/solution.py
+++ b/solution.py
@@ -8,6 +8,18 @@
 MP = ("mp_0", "mp_1", "mp_2")
 TASK = ("task_0", "task_1")
 TASK_MP = ("task_0", "task_1", "mp_0", "mp_1", "mp_2")
+
+
+def turn_plate(vector, axis_tag):
+    return jnp.concatenate(
+        jax.lax.all_to_all(
+            jnp.stack([vector for _ in range(jax.lax.axis_size(axis_tag))]),
+            axis_name=axis_tag,
+            split_axis=0,
+            concat_axis=0,
+        ),
+        0,
+    )
 
 
 def cut_along(value, dim, length):
@@ -80,10 +92,7 @@
     back = rotate(2.0 * scale * live * err, cosine, sine, -1.0, HEAD).astype(jnp.bfloat16)
     block = columns
     local_grad = lax.dot_general(
-        block,
-        lax.all_gather(back, MP, axis=0, tiled=True),
-        (((0,), (0,)), ((), ())),
-        preferred_element_type=jnp.float32,
+        block, turn_plate(back, MP), (((0,), (0,)), ((), ())), preferred_element_type=jnp.float32
     )
     wgrad = lax.psum(local_grad, TASK)
     loss = by_axis(partial_loss, TASK_MP)

time: 392 us -> 424 us (1.082)
  blocking collectives: 125 us -> 225 us
  waiting for transfers between devices: 216 us -> 150 us
    all_to_all x0 -> x1, blocking collectives: none -> 103 us  [turn_plate(): jax.lax.all_to_all(jnp.stack([vector for _ in range(jax.lax.axis_size(axi...]
    all_gather x1 -> x0, waiting for transfers between devices: 64.3 us -> none  [local(): lax.all_gather(back, MP, axis=0, tiled=True)]
  transfers between devices with their start and end apart: 5 -> 4, of which waited for: 4 -> 3; matrix products, arithmetic and copies ran while one was open for 0% -> 0% of each run, Pallas kernels for 0% -> 0%
where the time goes in v1:
time: 424 us
  blocking collectives  225 us (53%)
  waiting for transfers between devices  150 us (35%)
  between operations  15.3 us (4%)
  other arithmetic  11.5 us (3%)
  starting transfers between devices  9.78 us (2%)
  local copies, waits for them, and re-layouts  7.71 us (2%)
  matrix products  4.76 us (1%)
    all_to_all x1, blocking collectives, turn_plate(): jax.lax.all_to_all(jnp.stack([vector for _ in range(jax.lax.axis_size(axi...  103 us
    psum x1, blocking collectives, local(): mixed = lax.psum(coeff[0] * tau_local, TASK)  81.8 us
    reduce_scatter x1, waiting for transfers between devices, scatter_pairs(): return lax.psum_scatter(tiles, chips, scatter_dimension=0, tiled=True)[0]  81.7 us
    psum x1, waiting for transfers between devices, local(): wgrad = lax.psum(local_grad, TASK)  48.3 us
    psum x5, blocking collectives, by_axis(): value = lax.psum(value, axis)  40.8 us
    reduce_scatter x1, waiting for transfers between devices, scatter_pairs(): tiles = lax.psum_scatter(tiles, core, scatter_dimension=0, tiled=True)  19.8 us
    all_to_all x1, starting transfers between devices, local(): lax.all_to_all(normed, MP, split_axis=1, concat_axis=0, tiled=True)  9.66 us
  transfers between devices with their start and end apart: 4, of which 3 were waited for; matrix products, arithmetic and copies ran while one was open for 0% of the time, Pallas kernels for 0%

profile of v1, /device:TPU:32, one launch (start us, length us, event | category | flops | bytes accessed | tf_op | source)
XLA Modules:
  0.0 423.9 jit_solution(17464864771849105129)
XLA Ops:
  7.2 1.5 multiply_reduce_fusion
  8.7 1.6 copy.10
  10.3 2.2 fusion.1
  12.6 9.7 %all-to-all-start = ((bf16[64,32,256]{2,0,1:T(8,128)(2,1)}), bf16[64,32,256]{2,0,1:T(8,128)(2,1)S(1)}, u32[]{:S(2)}, u32[]{:S(2)}) async-start(bf16[64,32,256]{2,0,1:T(8,128)(2,1)} %fusion.1), calls=%async_computation | async-start | bytes 2097152 | tf_op jit(solution)/shard_map/all_to_all | solution.py:72
  22.3 1.4 convert_multiply_fusion
  23.6 81.8 %all-reduce.4 = bf16[256,1024]{1,0:T(8,128)(2,1)S(1)} all-reduce(f32[256,1024]{1,0:T(8,128)S(1)} %convert_multiply_fusion), channel_id=1, replica_groups=mesh['task_0'=2,'task_1'=4,'mp_0'=2,'mp_1'=8,'mp_2'=2] {'task_0','task_1'}, use_global_device_ids=true, to_apply=%region_1.0 | all-reduce | flops 262144 | bytes 1572864 | tf_op jit(solution)/shard_map/psum | solution.py:74
  105.5 1.3 fusion.9
  106.7 1.3 convolution_subtract_fusion
  108.0 4.1 copy.9
  112.2 19.8 %reduce-scatter.3.cloned.1.call-done = f32[16,64,1024]{2,1,0:T(8,128)} async-done(((f32[32,64,1024]{2,1,0:T(8,128)}), f32[16,64,1024]{2,1,0:T(8,128)}) %reduce-scatter.3.cloned.1.call-update) | async-done | bytes 4194320 | tf_op jit(solution)/shard_map/reduce_scatter | solution.py:35
  133.0 81.7 %reduce-scatter.5.cloned.1.call-done = f32[1,64,1024]{2,1,0:T(8,128)} async-done(((f32[16,64,1024]{2,1,0:T(8,128)}), f32[1,64,1024]{2,1,0:T(8,128)}) %reduce-scatter.5.cloned.1.call-update) | async-done | bytes 262160 | tf_op jit(solution)/shard_map/reduce_scatter | solution.py:36
  214.7 1.3 reshape_squeeze.3
  216.6 1.8 fusion.5
  218.4 0.7 subtract_convert_fusion
  219.1 0.7 pad_maximum_fusion.1
  220.5 102.5 %all_to_all.21 = bf16[32,64,1024]{2,1,0:T(8,128)(2,1)S(1)} all-to-all(bf16[32,64,1024]{2,1,0:T(8,128)(2,1)S(1)} %stack.9), channel_id=1, replica_groups=mesh['task_0'=2,'task_1'=4,'mp_0'=2,'mp_1'=8,'mp_2'=2] {'mp_0','mp_1','m..., dimensions={0} | all-to-all | bytes 8388608 | tf_op jit(solution)/shard_map/all_to_all | solution.py:15
  323.0 2.3 convolution_bitcast_fusion
  325.9 6.9 %psum.51 = f32[]{:T(128)} all-reduce(f32[]{:T(128)S(6)} %mul.221), channel_id=1, replica_groups=mesh['task_0'=2,'task_1'=4,'mp_0'=2,'mp_1'=8,'mp_2'=2] {'task_0'}, use_global_device_ids=true, to_apply=%region_6.0 | all-reduce | flops 1 | bytes 8 | tf_op jit(solution)/shard_map/psum | solution.py:41
  332.9 10.8 %psum.52 = f32[]{:T(128)} all-reduce(f32[]{:T(128)} %psum.51), channel_id=1, replica_groups=mesh['task_0'=2,'task_1'=4,'mp_0'=2,'mp_1'=8,'mp_2'=2] {'task_1'}, use_global_device_ids=true, to_apply=%region_7.0 | all-reduce | flops 1 | bytes 8 | tf_op jit(solution)/shard_map/psum | solution.py:41
  343.7 5.5 %psum.53 = f32[]{:T(128)} all-reduce(f32[]{:T(128)} %psum.52), channel_id=1, replica_groups=mesh['task_0'=2,'task_1'=4,'mp_0'=2,'mp_1'=8,'mp_2'=2] {'mp_0'}, use_global_device_ids=true, to_apply=%region_8.0 | all-reduce | flops 1 | bytes 8 | tf_op jit(solution)/shard_map/psum | solution.py:41
  349.2 14.4 %psum.54 = f32[]{:T(128)} all-reduce(f32[]{:T(128)} %psum.53), channel_id=1, replica_groups=mesh['task_0'=2,'task_1'=4,'mp_0'=2,'mp_1'=8,'mp_2'=2] {'mp_1'}, use_global_device_ids=true, to_apply=%region_9.0 | all-reduce | flops 1 | bytes 8 | tf_op jit(solution)/shard_map/psum | solution.py:41
  363.6 3.1 psum.55
  366.7 48.3 %all-reduce.3.cloned.1.call-done = f32[256,1024]{1,0:T(8,128)} async-done(((f32[256,1024]{1,0:T(8,128)}), f32[256,1024]{1,0:T(8,128)}) %all-reduce.3.cloned.1.call-update) | async-done | bytes 1048592 | tf_op jit(solution)/shard_map/psum | solution.py:97
  415.0 2.4 fusion.3
  (23 shorter events, 1.7 us)
Async XLA Ops:
  7.2 3.1 copy-start.1
  8.7 13.6 %copy-start = (bf16[1,256,1024]{2,1,0:T(8,128)(2,1)S(1)}, bf16[1,256,1024]{2,1,0:T(8,128)(2,1)}, u32[]{:S(2)}) copy-start(bf16[1,256,1024]{2,1,0:T(8,128)(2,1)} %param.8) | copy-start | bytes 1572868
  12.6 92.9 %all-to-all-start = ((bf16[64,32,256]{2,0,1:T(8,128)(2,1)}), bf16[64,32,256]{2,0,1:T(8,128)(2,1)S(1)}, u32[]{:S(2)}, u32[]{:S(2)}) async-start(bf16[64,32,256]{2,0,1:T(8,128)(2,1)} %fusion.1), calls=%async_computation | async-start | bytes 2097152 | tf_op jit(solution)/shard_map/all_to_all | solution.py:72
  22.2 109.8 %reduce-scatter.3.cloned.1.call-start = ((), (), s32[]{:S(2)}) async-start(), calls=%async_computation.4 | async-start | bytes 12582912 | tf_op jit(solution)/shard_map/reduce_scatter | solution.py:35
  112.1 20.7 %copy-start.2 = (s32[1,64]{1,0:T(1,128)S(1)}, s32[1,64]{1,0:T(1,128)}, u32[]{:S(2)}) copy-start(s32[1,64]{1,0:T(1,128)} %param.11) | copy-start | bytes 772
  112.1 102.6 %reduce-scatter.5.cloned.1.call-start = ((), (), s32[]{:S(2)}) async-start(), calls=%async_computation.5 | async-start | bytes 4456448 | tf_op jit(solution)/shard_map/reduce_scatter | solution.py:36
  132.0 283.0 %all-reduce.3.cloned.1.call-start = ((), (), s32[]{:S(2)}) async-start(), calls=%async_computation.6 | async-start | bytes 2097152 | tf_op jit(solution)/shard_map/psum | solution.py:97
Sparse Core Ops, SparseCore 0:
  112.2 19.7 reduce-scatter.2
  134.5 80.0 reduce-scatter.4
  325.4 89.5 all-reduce.2
